TPU v7x, 32 devices: a whole 2x2x4 slice. The times are simulated.
32 devices in a mesh: groups: 2 (over x), gx: 8 (over z, y), gy: 2 (over core).
Axes of the slice: x: 2, y: 2, z: 4, core: 2. Of those that a mesh axis runs over, the one named last changes fastest.
Arguments:
- tokens: bfloat16 [64, 16384], P('groups', 'gx'), parts along dimension 0, may hold values from -6 to 6
- w_query: bfloat16 [16384, 8192], P('gx', 'gy'), may hold values from -0.046875 to 0.046875
- w_key: bfloat16 [16384, 512], P('gx', 'gy'), may hold values from -0.046875 to 0.046875
- w_value: bfloat16 [16384, 512], P('gx', 'gy'), may hold values from -0.046875 to 0.046875
- w_out: bfloat16 [8192, 16384], P('gy', 'gx'), may hold values from -0.0625 to 0.0625
- key_cache: bfloat16 [64, 4, 1024, 128], P(('groups', 'gx'), 'gy'), parts along dimension 0, may hold values from -600 to 600
- value_cache: bfloat16 [64, 4, 1024, 128], P(('groups', 'gx'), 'gy'), parts along dimension 0, may hold values from -6 to 6
- lengths: int32 [64], P(('groups', 'gx')), parts along dimension 0, may hold values from 2 to 1024, as said below
Outputs:
- attended: bfloat16 [64, 16384], P(('groups', 'gy'), 'gx'), parts along dimension 0
There are 2 independent parts, one for each index of `groups`. A program takes and returns all parts, laid end to end along the dimension named above; an argument that names none is the same for every part. Nothing has to cross between parts.
Inputs may be any that keep to these rules, and one draw needn't show every extreme that they name: `lengths`: every row has 2 or more filled slots; some row has all 1024 slots filled.
All inputs are finite; a program needn't handle non-finite values.
Results may differ from a plain program's by a relative error of at most 0.011.
Values may be sent and summed in bfloat16 or wider, within the bound.
A program may use at most 128 MiB of HBM per device.

v0:
```python
import jax
import jax.numpy as jnp
from jax import lax
from jax.sharding import PartitionSpec as P

rope_base = 500000.0


def rotate(vectors, positions):
    half = vectors.shape[-1] // 2
    freqs = rope_base ** (-2.0 * jnp.arange(half).astype(jnp.float32) / (2.0 * half))
    angles = positions[:, None] * freqs[None, :]
    cosine = jnp.cos(angles)[:, None, :]
    sine = jnp.sin(angles)[:, None, :]
    first = vectors[..., :half]
    second = vectors[..., half:]
    return jnp.concatenate(
        [first * cosine - second * sine, second * cosine + first * sine], axis=-1
    )


def on_device(tokens, w_query, w_key, w_value, w_out, key_cache, value_cache, lengths):
    rows_dev = key_cache.shape[0]
    kv_local = key_cache.shape[1]
    cache_slots = key_cache.shape[2]
    head_dim = key_cache.shape[3]
    query_cols = w_query.shape[1]
    kv_cols = w_key.shape[1]
    heads_local = query_cols // head_dim
    group = heads_local // kv_local

    def take_rows():
        return tokens

    queries = lax.psum_scatter(
        jnp.dot(take_rows(), w_query, preferred_element_type=jnp.float32),
        "gx",
        scatter_dimension=0,
        tiled=True,
    )
    picked = take_rows()
    key_values = lax.psum_scatter(
        jnp.concatenate(
            [
                jnp.dot(picked, w_key, preferred_element_type=jnp.float32),
                jnp.dot(picked, w_value, preferred_element_type=jnp.float32),
            ],
            axis=1,
        ),
        "gx",
        scatter_dimension=0,
        tiled=True,
    )
    keys_new = key_values[:, :kv_cols]
    values_new = key_values[:, kv_cols:]
    positions = lengths.astype(jnp.float32)
    queries_rot = rotate(queries.reshape(rows_dev, heads_local, head_dim), positions).astype(
        jnp.bfloat16
    )
    queries_rot = queries_rot.reshape(rows_dev, kv_local, group, head_dim)
    keys_rot = rotate(keys_new.reshape(rows_dev, kv_local, head_dim), positions).astype(
        jnp.bfloat16
    )
    values_b = values_new.astype(jnp.bfloat16).reshape(rows_dev, kv_local, head_dim)
    scaling = head_dim ** (-0.5)
    scores = (
        jnp.einsum("rkgd,rkcd->rkgc", queries_rot, key_cache, preferred_element_type=jnp.float32)
        * scaling
    )
    own_score = (
        jnp.einsum("rkgd,rkd->rkg", queries_rot, keys_rot, preferred_element_type=jnp.float32)
        * scaling
    )
    valid = jnp.arange(cache_slots)[None, :] < lengths[:, None]
    scores = jnp.where(valid[:, None, None, :], scores, jnp.float32(-1e30))
    highest = jnp.maximum(jnp.max(scores, axis=-1), own_score)
    weights = jnp.exp(scores - highest[..., None])
    own_weight = jnp.exp(own_score - highest)
    total = jnp.sum(weights, axis=-1) + own_weight
    probs = (weights / total[..., None]).astype(jnp.bfloat16)
    own_prob = (own_weight / total).astype(jnp.bfloat16)
    mixed = jnp.einsum("rkgc,rkcd->rkgd", probs, value_cache, preferred_element_type=jnp.float32)
    mixed = (
        mixed
        + own_prob.astype(jnp.float32)[..., None] * values_b.astype(jnp.float32)[:, :, None, :]
    )
    heads = mixed.astype(jnp.bfloat16).reshape(rows_dev, query_cols)
    terms = jnp.dot(
        lax.all_gather(heads, "gx", axis=0, tiled=True), w_out, preferred_element_type=jnp.float32
    )
    return lax.psum_scatter(terms, "gy", scatter_dimension=0, tiled=True).astype(jnp.bfloat16)


def solution(mesh):
    in_specs = (
        P("groups", "gx"),
        P("gx", "gy"),
        P("gx", "gy"),
        P("gx", "gy"),
        P("gy", "gx"),
        P(("groups", "gx"), "gy", None, None),
        P(("groups", "gx"), "gy", None, None),
        P(("groups", "gx")),
    )
    out_specs = P(("groups", "gy"), "gx")
    return jax.shard_map(
        on_device, mesh=mesh, in_specs=in_specs, out_specs=out_specs, check_vma=False
    )
```

profile of v0, /device:TPU:0, one launch (start us, length us, event | category | flops | bytes accessed | tf_op | source)
XLA Modules:
  0.0 155.5 jit_solution(17177970236067870084)
XLA Ops:
  6.5 0.0 copy-start
  6.5 0.0 all-reduce.5.cloned.1.call-start
  6.6 0.0 copy-start.3
  6.6 9.8 %fusion.13 = f32[32,4096]{1,0:T(8,128)} fusion(bf16[32,2048]{1,0:T(8,128)(2,1)} %param.8, bf16[2048,4096]{1,0:T(8,128)(2,1)} %param.9), kind=kOutput, calls=%fused_computation.35 | convolution fusion | flops 536870912 | bytes 17432576 | tf_op jit(solution)/shard_map/dot_general | solution.py:36
  16.4 0.0 copy-done.1
  16.4 0.0 copy-done.2
  16.4 0.3 fusion.14
  16.7 0.0 copy-done.3
  16.7 0.3 fusion.15
  17.0 0.6 pad_maximum_fusion
  17.6 0.0 all-reduce.5.cloned.1.call-update
  17.6 0.0 reduce-scatter.2.cloned.1.call-start
  17.7 0.6 dynamic-slice
  18.9 0.1 iota_compare_fusion
  19.0 0.1 multiply_cosine_fusion
  19.1 74.7 %all-reduce.5.cloned.1.call-done = (f32[32,4096]{1,0:T(8,128)}, f32[32,512]{1,0:T(8,128)}) async-done(((f32[32,4096]{1,0:T(8,128)}, f32[32,512]{1,0:T(8,128)}), (f32[32,4096]{1,0:T(8,128)}, f32[32,512]{1,0:T(8,128)})) %all-reduce.5.cloned.1.call-update) | async-done | bytes 589840
  93.8 0.7 constant_dynamic-slice_fusion
  94.5 0.9 dynamic-slice_bitcast_fusion
  95.4 0.1 subtract_convert_fusion.1
  95.5 0.1 subtract_convert_fusion
  95.6 0.1 maximum_bitcast_fusion
  95.7 0.2 fusion.5
  95.9 0.8 fusion.12
  96.7 0.2 fusion.2
  97.0 0.8 fusion.7
  97.8 2.0 %fusion.1 = bf16[4,2,16,128]{3,2,1,0:T(8,128)(2,1)S(1)} fusion(bf16[4,2,1024,128]{3,2,1,0:T(8,128)(2,1)} %param.14, f32[4,2,16,1024]{3,2,1,0:T(8,128)S(1)} %get-tuple-element.16, f32[4,2,16]{2,1,0:T(2,128)S(1)} %get-tuple-element.10, f32[4,2,16]{2,1,0:T(2,128)S(1)} %multiply_maximum_fusion, f32[4,2,128]{2,1,0:T(2,128)S(1)} %reshape.96, ...), kind=kOutput, calls=%fused_computation.3 | convolution fusion | flops 33996800 | bytes 2659840 | tf_op jit(solution)/shard_map/rkgc,rkcd->rkgd/dot_general | solution.py:82
  99.8 30.9 %all-gather = bf16[8,4,4096]{2,1,0:T(4,128)(2,1)S(1)} all-gather(bf16[1,4,4096]{2,1,0:T(4,128)(2,1)S(1)} %reshape.97), channel_id=1, replica_groups=mesh['groups'=2,'gx'=8,'gy'=2] {'gx'}, dimensions={0}, use_global_device_ids=true | all-gather | bytes 294912 | tf_op jit(solution)/shard_map/all_gather | solution.py:89
  130.7 0.1 reshape.98
  130.8 9.5 %fusion.16 = f32[32,2048]{1,0:T(8,128)} fusion(bf16[32,4096]{1,0:T(8,128)(2,1)S(1)} %reshape.98, bf16[4096,2048]{1,0:T(8,128)(2,1)} %param.12), kind=kOutput, calls=%fused_computation.38 | convolution fusion | flops 536870912 | bytes 17301504 | tf_op jit(solution)/shard_map/dot_general | solution.py:88
  140.3 0.0 reduce-scatter.2.cloned.1.call-update
  140.3 6.8 %reduce-scatter.2.cloned.1.call-done = f32[16,2048]{1,0:T(8,128)} async-done(((f32[32,2048]{1,0:T(8,128)}), f32[16,2048]{1,0:T(8,128)}) %reduce-scatter.2.cloned.1.call-update) | async-done | bytes 131088 | tf_op jit(solution)/shard_map/reduce_scatter | solution.py:91
  147.1 1.5 convert_element_type.48
  (15 shorter events, 0.1 us)
Async XLA Ops:
  6.5 89.4 %copy-start = (bf16[4,2,1024,128]{3,2,1,0:T(8,128)(2,1)S(1)}, bf16[4,2,1024,128]{3,2,1,0:T(8,128)(2,1)}, u32[]{:S(2)}) copy-start(bf16[4,2,1024,128]{3,2,1,0:T(8,128)(2,1)} %param.13) | copy-start | bytes 6291460
  6.5 11.2 %copy-start.5 = (u32[32]{0:T(128)S(1)}, u32[32]{0:T(128)}, u32[]{:S(2)}) copy-start(u32[32]{0:T(128)} %constant.21) | copy-start | bytes 388
  6.5 9.8 %copy-start.1 = (bf16[32,2048]{1,0:T(8,128)(2,1)S(1)}, bf16[32,2048]{1,0:T(8,128)(2,1)}, u32[]{:S(2)}) copy-start(bf16[32,2048]{1,0:T(8,128)(2,1)} %param.8) | copy-start | bytes 393220
  6.5 9.8 %copy-start.2 = (bf16[2048,256]{1,0:T(8,128)(2,1)S(1)}, bf16[2048,256]{1,0:T(8,128)(2,1)}, u32[]{:S(2)}) copy-start(bf16[2048,256]{1,0:T(8,128)(2,1)} %param.10) | copy-start | bytes 3145732
  6.5 11.1 %copy-start.4 = (s32[4]{0:T(128)S(1)}, s32[4]{0:T(128)}, u32[]{:S(2)}) copy-start(s32[4]{0:T(128)} %param.15) | copy-start | bytes 52
  6.5 87.2 %all-reduce.5.cloned.1.call-start = ((), (), s32[]{:S(2)}) async-start(), calls=%async_computation.2 | async-start | bytes 1179648
  6.6 10.1 %copy-start.3 = (bf16[2048,256]{1,0:T(8,128)(2,1)S(1)}, bf16[2048,256]{1,0:T(8,128)(2,1)}, u32[]{:S(2)}) copy-start(bf16[2048,256]{1,0:T(8,128)(2,1)} %param.11) | copy-start | bytes 3145732
  17.6 129.5 %reduce-scatter.2.cloned.1.call-start = ((), (), s32[]{:S(2)}) async-start(), calls=%async_computation.1 | async-start | bytes 393216 | tf_op jit(solution)/shard_map/reduce_scatter | solution.py:91
Sparse Core Ops, SparseCore 0:
  17.7 75.9 all-reduce.4
  140.4 6.6 reduce-scatter.1
where the time goes:
time: 156 us; the launch traced here: 155 us
  waiting for transfers between devices  81.6 us (52%)
  blocking collectives  30.9 us (20%)
  matrix products  22.8 us (15%)
  between operations  14.1 us (9%)
  other arithmetic  3.67 us (2%)
  local copies, waits for them, and re-layouts  2.35 us (2%)
    unnamed x3, waiting for transfers between devices  74.8 us
    all_gather x1, blocking collectives, on_device(): lax.all_gather(heads, 'gx', axis=0, tiled=True)  30.9 us
    dot_general x1, matrix products, on_device(): jnp.dot(take_rows(), w_query, preferred_element_type=jnp.float32)  9.76 us
    dot_general x1, matrix products, on_device(): jnp.dot(lax.all_gather(heads, 'gx', axis=0, tiled=True), w_out, preferred...  9.46 us
    reduce_scatter x1, waiting for transfers between devices, on_device(): lax.psum_scatter(terms, 'gy', scatter_dimension=0, tiled=True)  6.8 us
  transfers between devices with their start and end apart: 2, of which 2 were waited for; matrix products, arithmetic and copies ran while one was open for 0% of the time, Pallas kernels for 0%

commit v1 on v0

v1 whole, which is shorter than its diff:
```python
import functools

import jax
import jax.numpy as jnp
from jax import lax
from jax.experimental import pallas as pl
from jax.experimental.pallas import tpu as pltpu
from jax.sharding import PartitionSpec as P

rope_base = 500000.0
f32 = jnp.float32
bf16 = jnp.bfloat16
MESH = pl.DeviceIdType.MESH
LAG = 3


def inner_of(count):
    best = 1
    for size in range(1, count + 1):
        if count % size == 0 and size * size <= count:
            best = size
    return best


def kernel(
    outer, inner, lengths, freqs, tokens, w_query, w_key, w_value, w_out, key_cache, value_cache,
    out, wbuf, wob, kbuf, vbuf, part, got_a, sum_b, got_b, qs, ms, lhs32, lhs, gath, osum, ogot,
    wsem, wosem, csem, a_send, a_recv, b_send, b_recv, z_send, y_send, g_recv, o_send, o_recv,
):
    chunks, _, _, rows, width = part.shape
    count = outer * inner
    kv_cols = w_key.shape[1]
    kv_local, head_dim = kbuf.shape[1], kbuf.shape[3]
    slots = kbuf.shape[2]
    heads_local = qs.shape[1]
    group = heads_local // kv_local
    gcols = group * head_dim
    per_chunk = width // head_dim
    per_group = gcols // width
    me = lax.axis_index("gx")
    core = lax.axis_index("gy")
    o, i = me // inner, me % inner

    def along_z(d):
        return lax.rem(o + d, outer)

    def along_y(d):
        return lax.rem(i + d, inner)

    def q_copy(c):
        cols = pl.ds(pl.multiple_of((c - 1) * width, width), width)
        return pltpu.make_async_copy(w_query.at[:, cols], wbuf.at[c], wsem.at[c])

    k_copy = pltpu.make_async_copy(w_key, wbuf.at[0, :, pl.ds(0, kv_cols)], wsem.at[0])
    v_copy = pltpu.make_async_copy(w_value, wbuf.at[0, :, pl.ds(kv_cols, kv_cols)], wsem.at[chunks])
    kc_copy = pltpu.make_async_copy(key_cache, kbuf, csem.at[0])
    vc_copy = pltpu.make_async_copy(value_cache, vbuf, csem.at[1])
    wo_copies = [
        pltpu.make_async_copy(w_out.at[pl.ds(k * gcols, gcols)], wob.at[k], wosem.at[k])
        for k in range(kv_local)
    ]
    k_copy.start()
    v_copy.start()
    for c in range(1, chunks):
        q_copy(c).start()
    kc_copy.start()
    vc_copy.start()
    for copy in wo_copies:
        copy.start()

    barrier = pltpu.get_barrier_semaphore()
    for d in range(1, outer):
        pl.semaphore_signal(
            barrier, inc=1, device_id={"gx": along_z(d) * inner + i}, device_id_type=MESH
        )
    for d in range(1, inner):
        pl.semaphore_signal(
            barrier, inc=1, device_id={"gx": o * inner + along_y(d)}, device_id_type=MESH
        )
    pl.semaphore_signal(barrier, inc=1, device_id={"gy": 1 - core}, device_id_type=MESH)

    row_ids = lax.broadcasted_iota(jnp.int32, (rows, head_dim), 0)
    positions = jnp.zeros((rows, head_dim), jnp.int32)
    for r in range(rows):
        positions = jnp.where(row_ids == r, lengths[r], positions)
    angles = positions.astype(f32) * freqs[...]
    lanes = lax.broadcasted_iota(jnp.int32, (rows, head_dim), 1)
    cosine = jnp.cos(angles)
    sine = jnp.sin(angles)
    sine = jnp.where(lanes < head_dim // 2, -sine, sine)

    def rotate(x):
        return x * cosine + pltpu.roll(x, head_dim // 2, 1) * sine

    pl.semaphore_wait(barrier, outer - 1 + inner - 1 + 1)

    def a_copy(c, d):
        return pltpu.make_async_remote_copy(
            src_ref=part.at[c, along_y(d)],
            dst_ref=got_a.at[c, i],
            send_sem=a_send.at[c, d],
            recv_sem=a_recv.at[c, i],
            device_id={"gx": o * inner + along_y(d)},
            device_id_type=MESH,
        )

    def a_arrival(c, d):
        src = along_y(d)
        return pltpu.make_async_remote_copy(
            src_ref=got_a.at[c, src],
            dst_ref=got_a.at[c, src],
            send_sem=a_send.at[c, d],
            recv_sem=a_recv.at[c, src],
            device_id={"gx": o * inner + src},
            device_id_type=MESH,
        )

    def b_copy(c, d):
        return pltpu.make_async_remote_copy(
            src_ref=sum_b.at[c, along_z(d)],
            dst_ref=got_b.at[c, o],
            send_sem=b_send.at[c, d],
            recv_sem=b_recv.at[c, o],
            device_id={"gx": along_z(d) * inner + i},
            device_id_type=MESH,
        )

    def b_arrival(c, d):
        src = along_z(d)
        return pltpu.make_async_remote_copy(
            src_ref=got_b.at[c, src],
            dst_ref=got_b.at[c, src],
            send_sem=b_send.at[c, d],
            recv_sem=b_recv.at[c, src],
            device_id={"gx": src * inner + i},
            device_id_type=MESH,
        )

    def second_stage(c):
        total = part[c, i]
        for d in range(1, inner):
            a_arrival(c, d).wait_recv()
            total = total + got_a[c, along_y(d)]
        sum_b[c] = total
        for d in range(1, outer):
            b_copy(c, d).start()

    k_copy.wait()
    v_copy.wait()

    def project(c, carry):
        @pl.when(c > 0)
        def _():
            q_copy(c).wait()

        acc = jnp.dot(tokens[...], wbuf[c], preferred_element_type=f32)
        for p in range(count):
            part[c, p % inner, p // inner] = acc[p * rows : (p + 1) * rows, :]
        for d in range(1, inner):
            a_copy(c, d).start()

        @pl.when(c >= LAG)
        def _():
            second_stage(c - LAG)

        return carry

    lax.fori_loop(0, chunks, project, 0)
    for c in range(max(chunks - LAG, 0), chunks):
        second_stage(c)

    def reduced(c):
        total = sum_b[c, o]
        for d in range(1, outer):
            b_arrival(c, d).wait_recv()
            total = total + got_b[c, along_z(d)]
        return total

    key_values = reduced(0)
    keys_rot = [
        rotate(key_values[:, k * head_dim : (k + 1) * head_dim]).astype(bf16).astype(f32)
        for k in range(kv_local)
    ]
    values_b = [
        key_values[:, kv_cols + k * head_dim : kv_cols + (k + 1) * head_dim].astype(bf16).astype(f32)
        for k in range(kv_local)
    ]
    kc_copy.wait()
    vc_copy.wait()
    scaling = head_dim ** (-0.5)
    slot_ids = lax.broadcasted_iota(jnp.int32, (group, slots), 1)

    def g_copy(k, src_o, sem, target):
        return pltpu.make_async_remote_copy(
            src_ref=gath.at[k, i, src_o],
            dst_ref=gath.at[k, i, src_o],
            send_sem=sem,
            recv_sem=g_recv.at[k, i, src_o],
            device_id={"gx": target},
            device_id_type=MESH,
        )

    def g_arrival(k, src_i, src_o):
        return pltpu.make_async_remote_copy(
            src_ref=gath.at[k, src_i, src_o],
            dst_ref=gath.at[k, src_i, src_o],
            send_sem=z_send.at[k, 0],
            recv_sem=g_recv.at[k, src_i, src_o],
            device_id={"gx": lax.rem(me + 1, count)},
            device_id_type=MESH,
        )

    def forward(k, d):
        src = along_z(d)
        if d > 0:
            g_arrival(k, i, src).wait_recv()
        for e in range(1, inner):
            g_copy(k, src, y_send.at[k, d, e], o * inner + along_y(e)).start()

    for k in range(kv_local):
        for c in range(1 + k * per_group, 1 + (k + 1) * per_group):
            chunk = reduced(c)
            for h in range(per_chunk):
                qs[:, (c - 1) * per_chunk + h, :] = rotate(
                    chunk[:, h * head_dim : (h + 1) * head_dim]
                )
        for r in range(rows):
            query = qs[r, k * group : (k + 1) * group, :].astype(bf16)
            scores = (
                lax.dot_general(
                    query, kbuf[r, k], (((1,), (1,)), ((), ())), preferred_element_type=f32
                )
                * scaling
            )
            own = (
                jnp.sum(query.astype(f32) * keys_rot[k][r : r + 1, :], axis=-1, keepdims=True)
                * scaling
            )
            scores = jnp.where(slot_ids < lengths[r], scores, f32(-1e30))
            highest = jnp.maximum(jnp.max(scores, axis=-1, keepdims=True), own)
            weights = jnp.exp(scores - highest)
            own_weight = jnp.exp(own - highest)
            total = jnp.sum(weights, axis=-1, keepdims=True) + own_weight
            scale = 1.0 / total
            probs = (weights * scale).astype(bf16)
            own_prob = (own_weight * scale).astype(bf16).astype(f32)
            mixed = jnp.dot(probs, vbuf[r, k], preferred_element_type=f32)
            ms[r, k * group : (k + 1) * group, :] = mixed + own_prob * values_b[k][r : r + 1, :]
        for h in range(group):
            gath[k, i, o, :, h * head_dim : (h + 1) * head_dim] = ms[:, k * group + h, :].astype(
                bf16
            )
        for d in range(1, outer):
            g_copy(k, o, z_send.at[k, d], along_z(d) * inner + i).start()
        forward(k, 0)

    for k in range(kv_local):
        for d in range(1, outer):
            forward(k, d)

    tiles, _, half, tile = osum.shape

    def o_copy(j):
        return pltpu.make_async_remote_copy(
            src_ref=osum.at[j, 1 - core],
            dst_ref=ogot.at[j],
            send_sem=o_send.at[j],
            recv_sem=o_recv.at[j],
            device_id={"gy": 1 - core},
            device_id_type=MESH,
        )

    for k in range(kv_local):
        for e in range(1, inner):
            for d in range(outer):
                g_arrival(k, along_y(e), along_z(d)).wait_recv()
        for p in range(count):
            lhs32[p * rows : (p + 1) * rows, :] = gath[k, p % inner, p // inner].astype(f32)
        lhs[k] = lhs32[...].astype(bf16)
        wo_copies[k].wait()

        def multiply(j, carry):
            cols = pl.ds(pl.multiple_of(j * tile, tile), tile)
            term = jnp.dot(lhs[k], wob[k, :, cols], preferred_element_type=f32)
            if k > 0:
                term = term + osum[j].reshape(2 * half, tile)
            osum[j] = term.reshape(2, half, tile)
            if k == kv_local - 1:
                o_copy(j).start()
            return carry

        lax.fori_loop(0, tiles, multiply, 0)

    for j in range(tiles):
        o_copy(j).wait()
        out[:, j * tile : (j + 1) * tile] = (osum[j, core] + ogot[j]).astype(out.dtype)

    def drain(c, carry):
        for d in range(1, inner):
            a_copy(c, d).wait_send()
        for d in range(1, outer):
            b_copy(c, d).wait_send()
        return carry

    lax.fori_loop(0, chunks, drain, 0)
    for k in range(kv_local):
        for d in range(1, outer):
            g_copy(k, o, z_send.at[k, d], along_z(d) * inner + i).wait_send()
        for d in range(outer):
            for e in range(1, inner):
                g_copy(k, along_z(d), y_send.at[k, d, e], o * inner + along_y(e)).wait_send()


def on_device(count, tokens, w_query, w_key, w_value, w_out, key_cache, value_cache, lengths):
    rows, kv_local, slots, head_dim = key_cache.shape
    inner = inner_of(count)
    outer = count // inner
    batch, depth = tokens.shape
    query_cols = w_query.shape[1]
    width = 2 * w_key.shape[1]
    chunks = 1 + query_cols // width
    heads_local = query_cols // head_dim
    gcols = query_cols // kv_local
    out_cols = w_out.shape[1]
    tile = min(256, out_cols)
    tiles = out_cols // tile
    freqs = rope_base ** (-2.0 * jnp.arange(head_dim // 2).astype(f32) / head_dim)
    freqs = jnp.concatenate([freqs, freqs])[None, :]
    any_spec = pl.BlockSpec(memory_space=pl.ANY)
    vmem = pl.BlockSpec(memory_space=pltpu.VMEM)
    smem = pl.BlockSpec(memory_space=pltpu.SMEM)
    dma = pltpu.SemaphoreType.DMA
    return pl.pallas_call(
        functools.partial(kernel, outer, inner),
        out_shape=jax.ShapeDtypeStruct((batch // 2, out_cols), bf16),
        in_specs=[smem, vmem, vmem] + [any_spec] * 6,
        out_specs=vmem,
        scratch_shapes=[
            pltpu.VMEM((chunks, depth, width), bf16),
            pltpu.VMEM((kv_local, gcols, out_cols), bf16),
            pltpu.VMEM(key_cache.shape, bf16),
            pltpu.VMEM(value_cache.shape, bf16),
            pltpu.VMEM((chunks, inner, outer, rows, width), f32),
            pltpu.VMEM((chunks, inner, outer, rows, width), f32),
            pltpu.VMEM((chunks, outer, rows, width), f32),
            pltpu.VMEM((chunks, outer, rows, width), f32),
            pltpu.VMEM((rows, heads_local, head_dim), f32),
            pltpu.VMEM((rows, heads_local, head_dim), f32),
            pltpu.VMEM((batch, gcols), f32),
            pltpu.VMEM((kv_local, batch, gcols), bf16),
            pltpu.VMEM((kv_local, inner, outer, rows, gcols), bf16),
            pltpu.VMEM((tiles, 2, batch // 2, tile), f32),
            pltpu.VMEM((tiles, batch // 2, tile), f32),
            dma((chunks + 1,)),
            dma((kv_local,)),
            dma((2,)),
            dma((chunks, inner)),
            dma((chunks, inner)),
            dma((chunks, outer)),
            dma((chunks, outer)),
            dma((kv_local, outer)),
            dma((kv_local, outer, inner)),
            dma((kv_local, inner, outer)),
            dma((tiles,)),
            dma((tiles,)),
        ],
        compiler_params=pltpu.CompilerParams(
            collective_id=0, has_side_effects=True, vmem_limit_bytes=60 * 2**20
        ),
        name="decode_attention",
    )(lengths, freqs, tokens, w_query, w_key, w_value, w_out, key_cache, value_cache)


def solution(mesh):
    in_specs = (
        P("groups", "gx"),
        P("gx", "gy"),
        P("gx", "gy"),
        P("gx", "gy"),
        P("gy", "gx"),
        P(("groups", "gx"), "gy", None, None),
        P(("groups", "gx"), "gy", None, None),
        P(("groups", "gx")),
    )
    out_specs = P(("groups", "gy"), "gx")
    return jax.shard_map(
        functools.partial(on_device, mesh.shape["gx"]),
        mesh=mesh,
        in_specs=in_specs,
        out_specs=out_specs,
        check_vma=False,
    )
```

time: 156 us -> 36.5 us (0.23)
  waiting for transfers between devices: 81.6 us -> 0 us
  Pallas kernels: 0 us -> 34.2 us
  blocking collectives: 30.9 us -> 0 us
  matrix products: 22.8 us -> 0 us
  between operations: 14.1 us -> 0.01 us
  other arithmetic: 3.67 us -> 0.6 us
    unnamed x3 -> x0, waiting for transfers between devices: 74.8 us -> none
    pallas_call x0 -> x1, Pallas kernels: none -> 34.2 us  [on_device(): pl.pallas_call(functools.partial(kernel, outer, inner), out_shape=jax.Sha...]
    all_gather x1 -> x0, blocking collectives: 30.9 us -> none  [on_device(): lax.all_gather(heads, 'gx', axis=0, tiled=True)]
    dot_general x7 -> x0, matrix products: 22.8 us -> none  [the longest x1 9.76 us: on_device(): jnp.dot(take_rows(), w_query, preferred_element_type=jnp.float32)]
    reduce_scatter x1 -> x0, waiting for transfers between devices: 6.8 us -> none  [on_device(): lax.psum_scatter(terms, 'gy', scatter_dimension=0, tiled=True)]
    convert_element_type x4 -> x0, other arithmetic: 2.34 us -> none  [the longest x1 1.54 us: on_device(): lax.psum_scatter(terms, 'gy', scatter_dimension=0, tiled=True)]
  transfers between devices with their start and end apart: 2 -> 0, of which waited for: 2 -> 0; matrix products, arithmetic and copies ran while one was open for 0% -> 0% of each run, Pallas kernels for 0% -> 0%
where the time goes in v1:
time: 36.5 us; the launch traced here: 36.3 us
  Pallas kernels  34.2 us (94%)
  local copies, waits for them, and re-layouts  1.47 us (4%)
  other arithmetic  0.6 us (2%)
    pallas_call x1, Pallas kernels, on_device(): pl.pallas_call(functools.partial(kernel, outer, inner), out_shape=jax.Sha...  34.2 us
    unnamed x1, local copies, waits for them, and re-layouts  1.47 us

profile of v1, /device:TPU:0, one launch (start us, length us, event | category | flops | bytes accessed | tf_op | source)
XLA Modules:
  0.0 36.3 jit_solution(11881084009935883513)
XLA Ops:
  0.0 0.6 %maximum_bitcast_fusion.freqs = f32[1,128]{1,0:T(1,128)} fusion(f32[64]{0:T(128)S(1)} %multiply_power_fusion), kind=kLoop, calls=%fused_computation | loop fusion | flops 128 | bytes 768 | tf_op jit(solution)/shard_map/broadcast_in_dim | solution.py:328
  0.6 34.2 %decode_attention.1 = bf16[16,2048]{1,0:T(8,128)(2,1)} custom-call(s32[4]{0:T(128)} %lengths.1, f32[1,128]{1,0:T(1,128)} %maximum_bitcast_fusion.freqs, bf16[32,2048]{1,0:T(8,128)(2,1)} %tokens.1, bf16[2048,4096]{1,0:T(8,128)(2,1)} %w_query.1, bf16[2048,256]{1,0:T(8,128)(2,1)} %w_key.1, bf16[2048,256]{1,0:T(8,128)(2,1)} %w_value.1, ...), custom_call_target="tpu_custom_call" | custom-call | tf_op jit(solution)/shard_map/decode_attention/pallas_call | solution.py:333
  34.8 1.5 %copy.10 = bf16[16,2048]{1,0:T(8,128)(2,1)} copy(bf16[16,2048]{1,0:T(8,128)(2,1)} %decode_attention.1) | data formatting | bytes 131072
  (1 shorter events, 0.0 us)

commit v2 on v1

--- a/solution.py
+++ b/solution.py
@@ -1,4 +1,5 @@
 import functools
+import math
 
 import jax
 import jax.numpy as jnp
@@ -11,7 +12,10 @@
 f32 = jnp.float32
 bf16 = jnp.bfloat16
 MESH = pl.DeviceIdType.MESH
-LAG = 3
+LAG = 5
+DEPTH = 6
+GREET = 0
+DIRECT = 8
 
 
 def inner_of(count):
@@ -23,8 +27,8 @@
 
 
 def kernel(
-    outer, inner, lengths, freqs, tokens, w_query, w_key, w_value, w_out, key_cache, value_cache,
-    out, wbuf, wob, kbuf, vbuf, part, got_a, sum_b, got_b, qs, ms, lhs32, lhs, gath, osum, ogot,
+    outer, inner, lengths, tokens, w_query, w_key, w_value, w_out, key_cache, value_cache,
+    out, tbuf, wbuf, wob, kbuf, vbuf, part, got_a, sum_b, got_b, qs, ms, lhs32, lhs, gath, osum, ogot,
     wsem, wosem, csem, a_send, a_recv, b_send, b_recv, z_send, y_send, g_recv, o_send, o_recv,
 ):
     chunks, _, _, rows, width = part.shape
@@ -55,36 +59,49 @@
     v_copy = pltpu.make_async_copy(w_value, wbuf.at[0, :, pl.ds(kv_cols, kv_cols)], wsem.at[chunks])
     kc_copy = pltpu.make_async_copy(key_cache, kbuf, csem.at[0])
     vc_copy = pltpu.make_async_copy(value_cache, vbuf, csem.at[1])
-    wo_copies = [
-        pltpu.make_async_copy(w_out.at[pl.ds(k * gcols, gcols)], wob.at[k], wosem.at[k])
-        for k in range(kv_local)
-    ]
+    pieces = wosem.shape[1]
+    piece = gcols // pieces
+
+    def wo_copy(k, t):
+        return pltpu.make_async_copy(
+            w_out.at[pl.ds(k * gcols + t * piece, piece)],
+            wob.at[k, pl.ds(t * piece, piece)],
+            wosem.at[k, t],
+        )
+
+    later = [kc_copy, vc_copy] + [wo_copy(k, t) for k in range(kv_local) for t in range(pieces)]
+    t_copy = pltpu.make_async_copy(tokens, tbuf, csem.at[2])
+    t_copy.start()
     k_copy.start()
     v_copy.start()
-    for c in range(1, chunks):
+    for c in range(1, min(DEPTH, chunks)):
         q_copy(c).start()
-    kc_copy.start()
-    vc_copy.start()
-    for copy in wo_copies:
-        copy.start()
 
     barrier = pltpu.get_barrier_semaphore()
-    for d in range(1, outer):
-        pl.semaphore_signal(
-            barrier, inc=1, device_id={"gx": along_z(d) * inner + i}, device_id_type=MESH
-        )
-    for d in range(1, inner):
-        pl.semaphore_signal(
-            barrier, inc=1, device_id={"gx": o * inner + along_y(d)}, device_id_type=MESH
-        )
+    direct = count <= DIRECT
+    if direct:
+        for d in range(1, count):
+            pl.semaphore_signal(
+                barrier, inc=1, device_id={"gx": lax.rem(me + d, count)}, device_id_type=MESH
+            )
+    else:
+        for d in range(1, outer):
+            pl.semaphore_signal(
+                barrier, inc=1, device_id={"gx": along_z(d) * inner + i}, device_id_type=MESH
+            )
+        for d in range(1, inner):
+            pl.semaphore_signal(
+                barrier, inc=1, device_id={"gx": o * inner + along_y(d)}, device_id_type=MESH
+            )
     pl.semaphore_signal(barrier, inc=1, device_id={"gy": 1 - core}, device_id_type=MESH)
 
     row_ids = lax.broadcasted_iota(jnp.int32, (rows, head_dim), 0)
     positions = jnp.zeros((rows, head_dim), jnp.int32)
     for r in range(rows):
         positions = jnp.where(row_ids == r, lengths[r], positions)
-    angles = positions.astype(f32) * freqs[...]
     lanes = lax.broadcasted_iota(jnp.int32, (rows, head_dim), 1)
+    index = lax.rem(lanes, head_dim // 2).astype(f32)
+    angles = positions.astype(f32) * jnp.exp(index * (-2.0 / head_dim * math.log(rope_base)))
     cosine = jnp.cos(angles)
     sine = jnp.sin(angles)
     sine = jnp.where(lanes < head_dim // 2, -sine, sine)
@@ -92,7 +109,8 @@
     def rotate(x):
         return x * cosine + pltpu.roll(x, head_dim // 2, 1) * sine
 
-    pl.semaphore_wait(barrier, outer - 1 + inner - 1 + 1)
+    greeted = count if direct else outer + inner - 1
+    greet_at = min(GREET, chunks - 1)
 
     def a_copy(c, d):
         return pltpu.make_async_remote_copy(
@@ -145,6 +163,7 @@
         for d in range(1, outer):
             b_copy(c, d).start()
 
+    t_copy.wait()
     k_copy.wait()
     v_copy.wait()
 
@@ -153,11 +172,30 @@
         def _():
             q_copy(c).wait()
 
-        acc = jnp.dot(tokens[...], wbuf[c], preferred_element_type=f32)
+        @pl.when(c + DEPTH < chunks)
+        def _():
+            q_copy(c + DEPTH).start()
+
+        for t, copy in enumerate(later[:DEPTH]):
+
+            @pl.when(c + DEPTH == chunks + t)
+            def _():
+                copy.start()
+
+        acc = jnp.dot(tbuf[...], wbuf[c], preferred_element_type=f32)
         for p in range(count):
             part[c, p % inner, p // inner] = acc[p * rows : (p + 1) * rows, :]
-        for d in range(1, inner):
-            a_copy(c, d).start()
+        @pl.when(c == greet_at)
+        def _():
+            pl.semaphore_wait(barrier, greeted)
+            for early in range(greet_at):
+                for d in range(1, inner):
+                    a_copy(early, d).start()
+
+        @pl.when(c >= greet_at)
+        def _():
+            for d in range(1, inner):
+                a_copy(c, d).start()
 
         @pl.when(c >= LAG)
         def _():
@@ -166,6 +204,8 @@
         return carry
 
     lax.fori_loop(0, chunks, project, 0)
+    for copy in later[DEPTH:]:
+        copy.start()
     for c in range(max(chunks - LAG, 0), chunks):
         second_stage(c)
 
@@ -250,11 +290,18 @@
             gath[k, i, o, :, h * head_dim : (h + 1) * head_dim] = ms[:, k * group + h, :].astype(
                 bf16
             )
-        for d in range(1, outer):
-            g_copy(k, o, z_send.at[k, d], along_z(d) * inner + i).start()
-        forward(k, 0)
-
-    for k in range(kv_local):
+        if direct:
+            for d in range(1, outer):
+                for e in range(inner):
+                    g_copy(k, o, y_send.at[k, d, e], along_z(d) * inner + along_y(e)).start()
+            for e in range(1, inner):
+                g_copy(k, o, y_send.at[k, 0, e], o * inner + along_y(e)).start()
+        else:
+            for d in range(1, outer):
+                g_copy(k, o, z_send.at[k, d], along_z(d) * inner + i).start()
+            forward(k, 0)
+
+    for k in range(0 if direct else kv_local):
         for d in range(1, outer):
             forward(k, d)
 
@@ -271,13 +318,15 @@
         )
 
     for k in range(kv_local):
-        for e in range(1, inner):
+        for e in range(inner):
             for d in range(outer):
-                g_arrival(k, along_y(e), along_z(d)).wait_recv()
+                if e > 0 or (direct and d > 0):
+                    g_arrival(k, along_y(e), along_z(d)).wait_recv()
         for p in range(count):
             lhs32[p * rows : (p + 1) * rows, :] = gath[k, p % inner, p // inner].astype(f32)
         lhs[k] = lhs32[...].astype(bf16)
-        wo_copies[k].wait()
+        for t in range(pieces):
+            wo_copy(k, t).wait()
 
         def multiply(j, carry):
             cols = pl.ds(pl.multiple_of(j * tile, tile), tile)
@@ -304,10 +353,11 @@
 
     lax.fori_loop(0, chunks, drain, 0)
     for k in range(kv_local):
-        for d in range(1, outer):
-            g_copy(k, o, z_send.at[k, d], along_z(d) * inner + i).wait_send()
+        if not direct:
+            for d in range(1, outer):
+                g_copy(k, o, z_send.at[k, d], along_z(d) * inner + i).wait_send()
         for d in range(outer):
-            for e in range(1, inner):
+            for e in range(0 if direct and d > 0 else 1, inner):
                 g_copy(k, along_z(d), y_send.at[k, d, e], o * inner + along_y(e)).wait_send()
 
 
@@ -324,8 +374,6 @@
     out_cols = w_out.shape[1]
     tile = min(256, out_cols)
     tiles = out_cols // tile
-    freqs = rope_base ** (-2.0 * jnp.arange(head_dim // 2).astype(f32) / head_dim)
-    freqs = jnp.concatenate([freqs, freqs])[None, :]
     any_spec = pl.BlockSpec(memory_space=pl.ANY)
     vmem = pl.BlockSpec(memory_space=pltpu.VMEM)
     smem = pl.BlockSpec(memory_space=pltpu.SMEM)
@@ -333,9 +381,10 @@
     return pl.pallas_call(
         functools.partial(kernel, outer, inner),
         out_shape=jax.ShapeDtypeStruct((batch // 2, out_cols), bf16),
-        in_specs=[smem, vmem, vmem] + [any_spec] * 6,
+        in_specs=[smem] + [any_spec] * 7,
         out_specs=vmem,
         scratch_shapes=[
+            pltpu.VMEM(tokens.shape, bf16),
             pltpu.VMEM((chunks, depth, width), bf16),
             pltpu.VMEM((kv_local, gcols, out_cols), bf16),
             pltpu.VMEM(key_cache.shape, bf16),
@@ -352,8 +401,8 @@
             pltpu.VMEM((tiles, 2, batch // 2, tile), f32),
             pltpu.VMEM((tiles, batch // 2, tile), f32),
             dma((chunks + 1,)),
-            dma((kv_local,)),
-            dma((2,)),
+            dma((kv_local, 4)),
+            dma((3,)),
             dma((chunks, inner)),
             dma((chunks, inner)),
             dma((chunks, outer)),
@@ -368,7 +417,7 @@
             collective_id=0, has_side_effects=True, vmem_limit_bytes=60 * 2**20
         ),
         name="decode_attention",
-    )(lengths, freqs, tokens, w_query, w_key, w_value, w_out, key_cache, value_cache)
+    )(lengths, tokens, w_query, w_key, w_value, w_out, key_cache, value_cache)
 
 
 def solution(mesh):

time: 36.5 us -> 33.6 us (0.921)
  Pallas kernels: 34.2 us -> 32 us
  other arithmetic: 0.6 us -> 0 us
    pallas_call x1, Pallas kernels: 34.2 us -> 32 us  [on_device(): pl.pallas_call(functools.partial(kernel, outer, inner), out_shape=jax.Sha...]
    broadcast_in_dim x1 -> x0, other arithmetic: 0.59 us -> none  [on_device(): freqs = jnp.concatenate([freqs, freqs])[None, :]]
where the time goes in v2:
time: 33.6 us; the launch traced here: 33.5 us
  Pallas kernels  32 us (95%)
  local copies, waits for them, and re-layouts  1.47 us (4%)
    pallas_call x1, Pallas kernels, on_device(): pl.pallas_call(functools.partial(kernel, outer, inner), out_shape=jax.Sha...  32 us
    unnamed x1, local copies, waits for them, and re-layouts  1.47 us

profile of v2, /device:TPU:0, one launch (start us, length us, event | category | flops | bytes accessed | tf_op | source)
XLA Modules:
  0.0 33.5 jit_solution(5197967393578315190)
XLA Ops:
  0.0 32.0 %decode_attention.1 = bf16[16,2048]{1,0:T(8,128)(2,1)} custom-call(s32[4]{0:T(128)} %lengths.1, bf16[32,2048]{1,0:T(8,128)(2,1)} %tokens.1, bf16[2048,4096]{1,0:T(8,128)(2,1)} %w_query.1, bf16[2048,256]{1,0:T(8,128)(2,1)} %w_key.1, bf16[2048,256]{1,0:T(8,128)(2,1)} %w_value.1, bf16[4096,2048]{1,0:T(8,128)(2,1)} %w_out.1, ...), custom_call_target="tpu_custom_call" | custom-call | tf_op jit(solution)/shard_map/decode_attention/pallas_call | solution.py:381
  32.0 1.5 %copy.10 = bf16[16,2048]{1,0:T(8,128)(2,1)} copy(bf16[16,2048]{1,0:T(8,128)(2,1)} %decode_attention.1) | data formatting | bytes 131072
